TPU v7x, 128 devices: a whole 4x4x4 slice. The times are simulated.
128 devices in a mesh: row: 4 (over z), col: 16 (over x_hi, y, core), smp: 2 (over x_lo).
Axes of the slice: x: 4 (x_hi: 2, x_lo: 2; x = x_hi * 2 + x_lo), y: 4, z: 4, core: 2. Of those that a mesh axis runs over, the one named last changes fastest.
Arguments:
- pair_repr: bfloat16 [512, 512, 128], P('row', 'col'), may hold values from -6 to 6
- tri_weight: bfloat16 [128, 512], replicated, may hold values from -0.75 to 0.75
- tri_bias_weight: bfloat16 [128, 4], replicated, may hold values from -40 to 40
- tri_output_weight: bfloat16 [128, 128], replicated, may hold values from -0.5 to 0.5
- samples: bfloat16 [8, 512, 768], P('smp'), may hold values from -6 to 6
- levels: int32 [8], P('smp'), may hold values from 0 to 199
- single_cond: bfloat16 [512, 384], replicated, may hold values from -6 to 6
- noise_weight: bfloat16 [256, 384], replicated, may hold values from -0.375 to 0.375
- modulation_weight: bfloat16 [384, 1536], replicated, may hold values from -0.3125 to 0.3125
- attention_weight: bfloat16 [768, 3072], replicated, may hold values from -0.5 to 0.5
- pair_bias_weight: bfloat16 [128, 16], replicated, may hold values from -40 to 40
- output_weight: bfloat16 [768, 768], replicated, may hold values from -0.21875 to 0.21875
- output_gate_weight: bfloat16 [384, 768], replicated, may hold values from -0.3125 to 0.3125
Outputs:
- new_pair: bfloat16 [512, 512, 128], P('row', 'col')
- attn_update: bfloat16 [8, 512, 768], P('smp', ('row', 'col'))
All inputs are finite; a program needn't handle non-finite values.
Results may differ from a plain program's by a relative error of at most 0.02.
The roundings to bfloat16 on the way count: a program that leaves them out, or rounds other values in their place, can miss the bound.
Values may be sent and summed in bfloat16 or wider, within the bound.
A program may use at most 128 MiB of HBM per device.

v0:
```python
import math

import jax
import jax.numpy as jnp
from jax import lax
from jax.sharding import PartitionSpec as P

HT = 4
DT = 32
CA = 768
HD = 16
DH = 48
NE = 256
LEVELS = 200


NORM_EPSILON = 1e-05
SIGMA_DATA = 16.0
SIGMA_MAX = 160.0
SIGMA_MIN = 0.0004


def combined_all(part, axis, combine):
    gathered = jax.tree.map(lambda a: lax.all_gather(a, axis), part)

    def take(source):
        return jax.tree.map(lambda a: lax.dynamic_index_in_dim(a, source, 0, False), gathered)

    return lax.fori_loop(
        1, lax.axis_size(axis), lambda source, state: combine(state, take(source)), take(0)
    )


def normalize(values):
    values = values.astype(jnp.float32)
    average = jnp.mean(values, axis=-1, keepdims=True)
    centred = values - average
    variance = jnp.mean(centred * centred, axis=-1, keepdims=True)
    return centred * lax.rsqrt(variance + NORM_EPSILON)


def noise_features(levels):
    fraction = levels.astype(jnp.float32) / (LEVELS - 1)
    upper_root = SIGMA_MAX ** (1.0 / 7.0)
    lower_root = SIGMA_MIN ** (1.0 / 7.0)
    noise_sigma = SIGMA_DATA * (upper_root + fraction * (lower_root - upper_root)) ** 7
    scaled = 0.25 * jnp.log(noise_sigma / SIGMA_DATA)
    frequency = (
        2.0
        * math.pi
        * jnp.exp(jnp.arange(NE // 2, dtype=jnp.float32) * (math.log(100.0) / (NE // 2)))
    )
    angles = scaled[:, None] * frequency[None, :]
    return jnp.concatenate([jnp.cos(angles), jnp.sin(angles)], axis=-1)


def attend_columns(pair_cols, bias_full, tri_weight, tri_output_weight):
    row_count, col_count, channels = pair_cols.shape
    normed = normalize(pair_cols).astype(jnp.bfloat16)
    projected = jnp.dot(
        normed.reshape(row_count * col_count, channels),
        tri_weight,
        preferred_element_type=jnp.float32,
    )
    projected = projected.reshape(row_count, col_count, 4, HT * DT)
    query_part = (projected[:, :, 0] * DT ** (-0.5)).astype(jnp.bfloat16)
    key_part = projected[:, :, 1].astype(jnp.bfloat16)
    value_part = projected[:, :, 2].astype(jnp.bfloat16)
    gate_part = projected[:, :, 3]

    def one_column(column):
        query_col = lax.dynamic_index_in_dim(query_part, column, 1, keepdims=False).reshape(
            row_count, HT, DT
        )
        key_col = lax.dynamic_index_in_dim(key_part, column, 1, keepdims=False).reshape(
            row_count, HT, DT
        )
        value_col = lax.dynamic_index_in_dim(value_part, column, 1, keepdims=False).reshape(
            row_count, HT, DT
        )
        gate_col = lax.dynamic_index_in_dim(gate_part, column, 1, keepdims=False)
        scores = jnp.einsum("ihd,khd->hik", query_col, key_col, preferred_element_type=jnp.float32)
        scores = scores + bias_full
        row_peak = jnp.max(scores, axis=-1, keepdims=True)
        exponent = jnp.exp(scores - row_peak)
        row_total = jnp.sum(exponent, axis=-1)
        attended = jnp.einsum(
            "hik,khd->ihd",
            exponent.astype(jnp.bfloat16),
            value_col,
            preferred_element_type=jnp.float32,
        )
        attended = attended / jnp.transpose(row_total)[:, :, None]
        return (jax.nn.sigmoid(gate_col) * attended.reshape(row_count, HT * DT)).astype(
            jnp.bfloat16
        )

    gated = lax.map(one_column, jnp.arange(col_count, dtype=jnp.int32))
    update = jnp.einsum("jic,cz->ijz", gated, tri_output_weight, preferred_element_type=jnp.float32)
    return (pair_cols.astype(jnp.float32) + update).astype(jnp.bfloat16)


def combine_parts(first, second):
    peak_one, total_one, sum_one = first
    peak_two, total_two, sum_two = second
    row_peak = jnp.maximum(peak_one, peak_two)
    factor_one = jnp.exp(peak_one - row_peak)
    factor_two = jnp.exp(peak_two - row_peak)
    row_total = total_one * factor_one + total_two * factor_two
    sample_count, token_count, channels = sum_one.shape
    head_count = row_peak.shape[1]

    def rescale(summed, factor):
        shaped = summed.reshape(sample_count, token_count, head_count, channels // head_count)
        return (shaped * jnp.transpose(factor, (0, 2, 1))[..., None]).reshape(
            sample_count, token_count, channels
        )

    return (row_peak, row_total, rescale(sum_one, factor_one) + rescale(sum_two, factor_two))


def local(
    pair_repr,
    tri_weight,
    tri_bias_weight,
    tri_output_weight,
    samples,
    levels,
    single_cond,
    noise_weight,
    modulation_weight,
    attention_weight,
    pair_bias_weight,
    output_weight,
    output_gate_weight,
):
    rows_here, cols_here, channels = pair_repr.shape
    col_count = lax.axis_size("col")
    row_index = lax.axis_index("row")
    col_index = lax.axis_index("col")
    normed_tile = normalize(pair_repr).astype(jnp.bfloat16)
    local_bias = jnp.einsum(
        "kiz,zh->hik", normed_tile, tri_bias_weight, preferred_element_type=jnp.float32
    )
    partial_bias = lax.all_gather(local_bias, "row", axis=2, tiled=True)
    bias_full = lax.all_gather(partial_bias, "col", axis=1, tiled=True)
    columns = lax.all_to_all(pair_repr, "row", split_axis=1, concat_axis=0, tiled=True)
    updated = attend_columns(columns, bias_full, tri_weight, tri_output_weight)
    new_tile = lax.all_to_all(updated, "row", split_axis=0, concat_axis=1, tiled=True)
    sample_count = samples.shape[0]
    own_count = rows_here // col_count
    own_start = col_index * own_count
    query_start = row_index * rows_here
    key_start = col_index * cols_here
    features = noise_features(levels).astype(jnp.bfloat16)
    noise_terms = jnp.dot(features, noise_weight, preferred_element_type=jnp.float32)

    def adapt(start, count):
        trunk = lax.dynamic_slice_in_dim(single_cond, start, count, 0).astype(jnp.float32)
        conditioned = normalize(trunk[None, :, :] + noise_terms[:, None, :]).astype(jnp.bfloat16)
        activation = lax.dynamic_slice_in_dim(samples, start, count, 1)
        modulation = jnp.einsum(
            "stc,cd->std", conditioned, modulation_weight, preferred_element_type=jnp.float32
        )
        adapted = (
            jax.nn.sigmoid(modulation[..., :CA]) * normalize(activation) + modulation[..., CA:]
        ).astype(jnp.bfloat16)
        return (conditioned, adapted)

    pair_renormed = normalize(new_tile).astype(jnp.bfloat16)
    pair_bias = jnp.einsum(
        "ikz,zh->hik", pair_renormed, pair_bias_weight, preferred_element_type=jnp.float32
    )
    cond_rows, adapted_rows = adapt(query_start, rows_here)
    cond_keys, adapted_keys = adapt(key_start, cols_here)
    query_part = jnp.einsum(
        "stc,cd->std", adapted_rows, attention_weight[:, :CA], preferred_element_type=jnp.float32
    )
    query_part = (
        (query_part * DH ** (-0.5)).astype(jnp.bfloat16).reshape(sample_count, rows_here, HD, DH)
    )
    key_value = jnp.einsum(
        "stc,cd->std",
        adapted_keys,
        attention_weight[:, CA : 3 * CA],
        preferred_element_type=jnp.float32,
    )
    key_part = key_value[..., :CA].astype(jnp.bfloat16).reshape(sample_count, cols_here, HD, DH)
    value_part = key_value[..., CA:].astype(jnp.bfloat16).reshape(sample_count, cols_here, HD, DH)
    scores = (
        jnp.einsum("sihd,skhd->shik", query_part, key_part, preferred_element_type=jnp.float32)
        + pair_bias[None]
    )
    adapted_own = lax.dynamic_slice_in_dim(adapted_rows, own_start, own_count, 1)
    cond_own = lax.dynamic_slice_in_dim(cond_rows, own_start, own_count, 1)
    local_peak = jnp.max(scores, axis=-1)
    exponent = jnp.exp(scores - local_peak[..., None])
    local_total = jnp.sum(exponent, axis=-1)
    partial_value = jnp.einsum(
        "shik,skhd->sihd",
        exponent.astype(jnp.bfloat16),
        value_part,
        preferred_element_type=jnp.float32,
    )
    partial_value = partial_value.reshape(sample_count, rows_here, CA)
    row_peak, row_total, summed = combined_all(
        (local_peak, local_total, partial_value), "col", combine_parts
    )
    row_total = lax.dynamic_slice_in_dim(row_total, own_start, own_count, 2)
    summed = lax.dynamic_slice_in_dim(summed, own_start, own_count, 1)
    attended = (
        summed.reshape(sample_count, own_count, HD, DH)
        / jnp.transpose(row_total, (0, 2, 1))[..., None]
    )
    attended = attended.reshape(sample_count, own_count, CA)
    gate_part = jnp.einsum(
        "stc,cd->std",
        adapted_own,
        attention_weight[:, 3 * CA :],
        preferred_element_type=jnp.float32,
    )
    gated = (jax.nn.sigmoid(gate_part) * attended).astype(jnp.bfloat16)
    projected_out = jnp.einsum(
        "stc,cd->std", gated, output_weight, preferred_element_type=jnp.float32
    )
    out_gate = jax.nn.sigmoid(
        jnp.einsum("stc,cd->std", cond_own, output_gate_weight, preferred_element_type=jnp.float32)
    )
    attn_update = (out_gate * projected_out).astype(jnp.bfloat16)
    return (new_tile, attn_update)


def solution(mesh):
    return jax.shard_map(
        local,
        mesh=mesh,
        in_specs=(
            P("row", "col", None),
            P(),
            P(),
            P(),
            P("smp", None, None),
            P("smp"),
            P(),
            P(),
            P(),
            P(),
            P(),
            P(),
            P(),
        ),
        out_specs=(P("row", "col", None), P("smp", ("row", "col"), None)),
        check_vma=False,
    )
```

profile of v0, /device:TPU:1, one launch (start us, length us, event | category | flops | bytes accessed | tf_op | source)
XLA Modules:
  0.0 460.5 jit_solution(10458823537242216250)
XLA Ops:
  13.5 12.3 %all_gather.21 = f32[4,32,512]{2,1,0:T(8,128)S(1)} all-gather(f32[4,32,128]{2,1,0:T(8,128)S(1)} %copy.113), channel_id=1, replica_groups=mesh['row'=4,'col'=16,'smp'=2] {'row'}, dimensions={2}, use_global_device_ids=true | all-gather | bytes 327680 | tf_op jit(solution)/shard_map/all_gather | solution.py:145
  28.1 3.8 all-to-all-start
  55.0 30.4 %all-gather.5.cloned.1.call-done = f32[4,512,512]{2,0,1:T(4,128)} async-done(((f32[4,32,512]{2,0,1:T(4,128)}), f32[4,512,512]{2,0,1:T(4,128)}) %all-gather.5.cloned.1.call-update) | async-done | bytes 4194320 | tf_op jit(solution)/shard_map/all_gather | solution.py:146
  85.4 5.2 %copy.119 = f32[4,512,512]{1,2,0:T(8,128)} copy(f32[4,512,512]{2,0,1:T(4,128)} %all-gather.5.cloned.1.call-done) | data formatting | bytes 8388608 | tf_op jit(solution)/shard_map/while | solution.py:98
  90.7 87.0 %while.29 = (s32[]{:T(128)}, bf16[8,512,128]{1,2,0:T(8,128)(2,1)}, s32[8]{0:T(128)S(1)}, f32[512,8,128]{2,0,1:T(8,128)}, bf16[512,8,128]{2,0,1:T(8,128)(2,1)}, /...) while((s32[]{:T(128)}, bf16[8,512,128]{1,2,0:T(8,128)(2,1)}, ...), condition=%wide.region_7.8_spmd, body=%wide.region_4.7_spmd.sunk | while | flops 140898304 | bytes 20750516 | solution.py:98
  96.6 3.0 fusion.174
  107.4 3.0 fusion.174
  118.3 3.0 fusion.174
  129.2 3.0 fusion.174
  140.1 3.0 fusion.174
  150.9 3.0 fusion.174
  161.8 3.0 fusion.174
  172.7 3.0 fusion.174
  181.1 4.1 all-to-all-start.1
  190.8 2.9 multiply_convert_fusion.2
  195.3 4.6 all-to-all-done.1
  203.2 2.9 convolution_bitcast_fusion
  211.0 24.7 %all-gather = f32[64,16,128]{2,1,0:T(8,128)S(1)} all-gather(f32[4,16,128]{2,1,0:T(8,128)S(1)} %get-tuple-element.335), channel_id=2, replica_groups=mesh['row'=4,'col'=16,'smp'=2] {'col'}, dimensions={0}, use_global_device_ids=true | all-gather | bytes 557056 | tf_op jit(solution)/shard_map/all_gather | solution.py:24
  236.0 22.1 %all-gather.1 = f32[64,16,128]{2,1,0:T(8,128)S(1)} all-gather(f32[4,16,128]{2,1,0:T(8,128)S(1)} %fusion.85), channel_id=3, replica_groups=mesh['row'=4,'col'=16,'smp'=2] {'col'}, dimensions={0}, use_global_device_ids=true | all-gather | bytes 557056 | tf_op jit(solution)/shard_map/all_gather | solution.py:24
  258.1 98.4 %all-gather.7.cloned.1.call-done = f32[16,4,128,768]{3,2,1,0:T(8,128)} async-done(((f32[1,4,128,768]{3,2,1,0:T(8,128)}), f32[16,4,128,768]{3,2,1,0:T(8,128)}) %all-gather.7.cloned.1.call-update) | async-done | bytes 25165840 | tf_op jit(solution)/shard_map/all_gather | solution.py:24
  359.7 88.7 %while.30 = (s32[]{:T(128)}, f32[4,16,128]{2,1,0:T(8,128)S(1)}, f32[4,16,128]{2,1,0:T(8,128)S(1)}, f32[4,128,768]{1,2,0:T(8,128)}, f32[16,4,16,128]{3,2,1,0:T(8,...) while((s32[]{:T(128)}, f32[4,16,128]{2,1,0:T(8,128)S(1)}, ...), condition=%wide.region_21.22_spmd, body=%wide.region_20.21_spmd.sunk | while | flops 1236997 | bytes 19890436 | solution.py:29
  368.7 2.9 fusion.179
  374.6 2.9 fusion.179
  380.5 2.9 fusion.179
  386.4 2.9 fusion.179
  392.3 2.9 fusion.179
  398.2 2.9 fusion.179
  404.1 2.9 fusion.179
  410.0 2.9 fusion.179
  415.9 2.9 fusion.179
  421.9 2.9 fusion.179
  427.8 2.9 fusion.179
  (400 shorter events, 162.6 us)
Async XLA Ops:
  7.2 33.0 %copy-start = (bf16[384,1536]{1,0:T(8,128)(2,1)S(1)}, bf16[384,1536]{1,0:T(8,128)(2,1)}, u32[]{:S(2)}) copy-start(bf16[384,1536]{1,0:T(8,128)(2,1)} %param.25) | copy-start | bytes 3538948
  7.2 4.4 copy-start.2
  7.2 4.4 copy-start.17
  7.2 78.2 %all-gather.5.cloned.1.call-start = ((), (), s32[]{:S(2)}) async-start(), calls=%async_computation.2 | async-start | bytes 4456448 | tf_op jit(solution)/shard_map/all_gather | solution.py:146
  26.7 5.3 %copy-start.13 = (bf16[128,512]{1,0:T(8,128)(2,1)S(1)}, bf16[128,512]{1,0:T(8,128)(2,1)}, u32[]{:S(2)}) copy-start(bf16[128,512]{1,0:T(8,128)(2,1)} %param.18) | copy-start | bytes 393220
  28.1 7.4 %copy-start.18 = (s32[4]{0:T(128)S(1)}, s32[4]{0:T(128)}, u32[]{:S(2)}) copy-start(s32[4]{0:T(128)} %param.22) | copy-start | bytes 52
  28.1 7.6 %copy-start.12 = (bf16[256,384]{1,0:T(8,128)(2,1)S(1)}, bf16[256,384]{1,0:T(8,128)(2,1)}, u32[]{:S(2)}) copy-start(bf16[256,384]{1,0:T(8,128)(2,1)} %param.24) | copy-start | bytes 589828
  28.1 16.9 %all-to-all-start = ((bf16[128,32,128]{2,0,1:T(8,128)(2,1)}), bf16[128,32,128]{2,0,1:T(8,128)(2,1)S(1)}, u32[]{:S(2)}, u32[]{:S(2)}) async-start(bf16[128,32,128]{2,0,1:T(8,128)(2,1)} %copy.110), calls=%async_computation | async-start | bytes 2097152 | tf_op jit(solution)/shard_map/all_to_all | solution.py:147
  33.1 7.5 %copy-start.11 = (bf16[768,3072]{1,0:T(8,128)(2,1)S(1)}, bf16[768,3072]{1,0:T(8,128)(2,1)}, u32[]{:S(2)}) copy-start(bf16[768,3072]{1,0:T(8,128)(2,1)} %param.26) | copy-start | bytes 14155780
  90.7 87.0 %copy-start.3 = (f32[128,4,8,128]{3,0,1,2:T(8,128)S(1)}, f32[128,4,8,128]{3,0,1,2:T(8,128)}, u32[]{:S(2)}) copy-start(f32[128,4,8,128]{3,0,1,2:T(8,128)} %copy.111) | copy-start | bytes 6291460
  90.7 87.0 %copy-start.14 = (bf16[128,128]{1,0:T(8,128)(2,1)S(1)}, bf16[128,128]{1,0:T(8,128)(2,1)}, u32[]{:S(2)}) copy-start(bf16[128,128]{1,0:T(8,128)(2,1)} %param.20) | copy-start | bytes 98308
  181.1 18.8 %all-to-all-start.1 = ((bf16[512,8,128]{2,1,0:T(8,128)(2,1)}), bf16[512,8,128]{2,1,0:T(8,128)(2,1)S(1)}, u32[]{:S(2)}, u32[]{:S(2)}) async-start(bf16[512,8,128]{2,1,0:T(8,128)(2,1)} %copy.121), calls=%async_computation.1 | async-start | bytes 2097152 | tf_op jit(solution)/shard_map/all_to_all | solution.py:149
  185.2 171.3 %all-gather.7.cloned.1.call-start = ((), (), s32[]{:S(2)}) async-start(), calls=%async_computation.3 | async-start | bytes 26738688 | tf_op jit(solution)/shard_map/all_gather | solution.py:24
  199.9 3.3 copy-start.16
  362.7 2.9 copy-start.6
  362.7 2.9 copy-start.9
  368.6 2.9 copy-start.6
  368.6 2.9 copy-start.9
  374.5 2.9 copy-start.6
  380.5 2.9 copy-start.6
  386.4 2.9 copy-start.6
  392.3 2.9 copy-start.6
  398.2 2.9 copy-start.6
  404.1 2.9 copy-start.6
  410.0 2.9 copy-start.6
  415.9 2.9 copy-start.6
  421.8 2.9 copy-start.6
  427.8 2.9 copy-start.6
  433.7 2.9 copy-start.6
  439.6 2.9 copy-start.6
  445.5 2.9 copy-start.6
  448.9 4.9 %copy-start.1 = (bf16[384,1536]{1,0:T(8,128)(2,1)S(1)}, bf16[384,1536]{1,0:T(8,128)(2,1)}, u32[]{:S(2)}) copy-start(bf16[384,1536]{1,0:T(8,128)(2,1)} %param.25) | copy-start | bytes 3538948
  (47 other events, 68.5 us)
Sparse Core Ops, SparseCore 0:
  26.8 58.5 all-gather.4
  209.9 146.5 all-gather.6
where the time goes:
time: 463 us; the launch traced here: 461 us
  waiting for transfers between devices  134 us (29%)
  local copies, waits for them, and re-layouts  103 us (22%)
  other arithmetic  77.4 us (17%)
  blocking collectives  59.1 us (13%)
  matrix products  49.2 us (11%)
  loops' own time  16.2 us (3%)
  between operations  14.5 us (3%)
  starting transfers between devices  8.01 us (2%)
    all_gather x1, waiting for transfers between devices, combined_all(): gathered = jax.tree.map(lambda a: lax.all_gather(a, axis), part)  98.4 us
    all_gather x2, blocking collectives, combined_all(): gathered = jax.tree.map(lambda a: lax.all_gather(a, axis), part)  46.8 us
    add x15, other arithmetic, combine_parts(): rescale(sum_one, factor_one) + rescale(sum_two, factor_two)  43.6 us
    all_gather x1, waiting for transfers between devices, local(): bias_full = lax.all_gather(partial_bias, 'col', axis=1, tiled=True)  30.4 us
    dynamic_slice x32, local copies, waits for them, and re-layouts, take(): lax.dynamic_index_in_dim(a, source, 0, False)  29.8 us
    dot_general x8, matrix products, one_column(): jnp.einsum('ihd,khd->hik', query_col, key_col, preferred_element_type=jnp...  23.6 us
    another operation x1, loops' own time, attend_columns(): gated = lax.map(one_column, jnp.arange(col_count, dtype=jnp.int32))  15.3 us
    while x135, local copies, waits for them, and re-layouts  13.6 us
  transfers between devices with their start and end apart: 4, of which 3 were waited for; matrix products, arithmetic and copies ran while one was open for 7% of the time, Pallas kernels for 0%

commit v1 on v0

v1 whole, which is shorter than its diff:
```python
import math

import jax
import jax.numpy as jnp
from jax import lax
from jax.experimental import pallas as pl
from jax.experimental.pallas import tpu as pltpu
from jax.sharding import PartitionSpec as P

MESH = pl.DeviceIdType.MESH
F32 = jnp.float32
BF16 = jnp.bfloat16

DT = 32
CA = 768
HD = 16
DH = 48
NE = 256
LEVELS = 200

NORM_EPSILON = 1e-05
SIGMA_DATA = 16.0
SIGMA_MAX = 160.0
SIGMA_MIN = 0.0004

NT = (((1,), (1,)), ((), ()))


def normalize(values):
    values = values.astype(F32)
    average = jnp.mean(values, axis=-1, keepdims=True)
    centred = values - average
    variance = jnp.mean(centred * centred, axis=-1, keepdims=True)
    return centred * lax.rsqrt(variance + NORM_EPSILON)


def noise_features(levels):
    fraction = levels.astype(F32) / (LEVELS - 1)
    upper_root = SIGMA_MAX ** (1.0 / 7.0)
    lower_root = SIGMA_MIN ** (1.0 / 7.0)
    noise_sigma = SIGMA_DATA * (upper_root + fraction * (lower_root - upper_root)) ** 7
    scaled = 0.25 * jnp.log(noise_sigma / SIGMA_DATA)
    frequency = 2.0 * math.pi * jnp.exp(jnp.arange(NE // 2, dtype=F32) * (math.log(100.0) / (NE // 2)))
    angles = scaled[:, None] * frequency[None, :]
    return jnp.concatenate([jnp.cos(angles), jnp.sin(angles)], axis=-1)


def sigmoid(x):
    return 1.0 / (1.0 + jnp.exp(-x))


def dot(a, b):
    return jnp.dot(a, b, preferred_element_type=F32)


def dot_nt(a, b):
    return lax.dot_general(a, b, NT, preferred_element_type=F32)


def kernel(
    noise,
    wtri,
    tbw,
    wo_big,
    pbw_big,
    pair_h,
    samples_h,
    cond_h,
    modw_h,
    attw_h,
    ow_h,
    ogw_h,
    new_out,
    upd_out,
    pair_v,
    f32buf,
    norm_t,
    loc,
    cols,
    bias,
    qbuf,
    kvbuf,
    gatebuf,
    resbuf,
    gbuf,
    grecv,
    renorm,
    pb_t,
    pb_recv,
    samples_v,
    cond_v,
    samp_own,
    cond_own,
    modw,
    attw,
    ow,
    ogw,
    kv_all,
    q_own,
    gate_own,
    og_own,
    att_all,
    lsem,
    ssem,
    rsem,
    gssem,
    grsem,
):
    r = lax.axis_index("row")
    c = lax.axis_index("col")
    s = lax.axis_index("smp")
    xh = c // 8
    y = (c // 2) % 4
    core = c % 2
    so = 1 - s
    c8 = (c + 8) % 16
    token = pl.multiple_of(r * 128 + c * 8, 8)

    barrier = pltpu.get_barrier_semaphore()

    def col_peer(d):
        b = (c + d) % 16
        return (r, b, (s + b // 8 + xh) % 2)

    def row_peer(d, e):
        return ((r + d) % 4, c, (s + e) % 2)

    greet = [row_peer(d, e) for d in range(4) for e in range(2) if d + e > 0]
    greet += [col_peer(d) for d in range(1, 16)]
    for peer in greet:
        pl.semaphore_signal(barrier, inc=1, device_id=peer, device_id_type=MESH)

    loads = [
        pltpu.make_async_copy(src, dst, lsem.at[n])
        for n, (src, dst) in enumerate(
            [
                (pair_h, pair_v),
                (cond_h, cond_v),
                (modw_h, modw),
                (samples_h, samples_v),
                (attw_h, attw),
                (samples_h.at[:, pl.ds(token, 8), :], samp_own),
                (cond_h.at[pl.ds(token, 8), :], cond_own),
                (ogw_h, ogw),
                (ow_h, ow),
            ]
        )
    ]
    for load in loads:
        load.start()

    loads[0].wait()

    def norm_step(t, carry):
        x = pair_v[pl.ds(t * 8, 8)].astype(F32).reshape(256, 128)
        f32buf[pl.ds(pl.multiple_of(t * 256, 256), 256), :] = normalize(x)
        return carry

    lax.fori_loop(0, 16, norm_step, 0)

    def turn_step(i, carry):
        v = f32buf[pl.ds(i, 128, stride=32), :].astype(BF16)
        norm_t[i] = v
        out = dot_nt(tbw[...], v)
        for h in range(4):
            loc[h, pl.ds(i, 1), :] = out[h : h + 1]
        return carry

    lax.fori_loop(0, 32, turn_step, 0)
    bias[c, r] = loc[pl.ds(2 * s, 2)]
    cols[r] = norm_t[pl.ds(8 * r, 8)]

    pl.semaphore_wait(barrier, len(greet))

    def send(n, src, dst, dev):
        return pltpu.make_async_remote_copy(
            src_ref=src,
            dst_ref=dst,
            send_sem=ssem.at[n],
            recv_sem=rsem.at[n],
            device_id=dev,
            device_id_type=MESH,
        )

    zp = ((r + 1) % 4, c, s)
    zm = ((r + 3) % 4, c, s)
    rm, rp = (r + 3) % 4, (r + 1) % 4

    def ycol(d):
        return xh * 8 + ((y + d) % 4) * 2 + core

    cp, c2, cm = ycol(1), ycol(2), ycol(3)
    cp8, c28, cm8 = (cp + 8) % 16, (c2 + 8) % 16, (cm + 8) % 16
    yp, ym = (r, cp, s), (r, cm, s)
    peer_core = (r, c + 1 - 2 * core, s)

    copies = {}
    copies[3] = send(3, loc.at[pl.ds(2 * so, 2)], bias.at[c, r], (r, c8, so))
    copies[4] = send(4, bias.at[c, r], bias.at[c, r], zp)
    copies[5] = send(5, bias.at[c, r], bias.at[c, r], zm)
    copies[6] = send(6, bias.at[c, rm], bias.at[c, rm], zp)
    copies[7] = send(7, bias.at[c8, r], bias.at[c8, r], zp)
    copies[8] = send(8, bias.at[c8, r], bias.at[c8, r], zm)
    copies[9] = send(9, bias.at[c8, rp], bias.at[c8, rp], zm)
    for n, unit, dev in (
        (10, c, yp),
        (11, c, ym),
        (12, cm, yp),
        (13, c8, yp),
        (14, c8, ym),
        (15, cp8, ym),
        (16, c, peer_core),
        (17, c8, peer_core),
        (18, cm, peer_core),
        (19, cp, peer_core),
        (20, c2, peer_core),
        (21, cm8, peer_core),
        (22, cp8, peer_core),
        (23, c28, peer_core),
    ):
        copies[n] = send(n, bias.at[unit], bias.at[unit], dev)
    for d in (1, 2, 3):
        dest = (r + d) % 4
        copies[d - 1] = send(d - 1, norm_t.at[pl.ds(8 * dest, 8)], cols.at[r], (dest, c, s))

    def start(*which):
        for n in which:
            copies[n].start()

    def arrived(*which):
        for n in which:
            copies[n].wait_recv()

    def kv_step(ch, carry):
        s4 = ch // 2
        t = pl.multiple_of((ch % 2) * 256, 256)
        trunk = cond_v[pl.ds(t, 256), :].astype(F32) + noise[pl.ds(s4, 1), :]
        m = dot(normalize(trunk).astype(BF16), modw[...])
        act = normalize(samples_v[s4, pl.ds(t, 256), :])
        ad = (sigmoid(m[:, :CA]) * act + m[:, CA:]).astype(BF16)
        at = pl.multiple_of(ch * 256, 256)
        kv_all[pl.ds(at, 256), :] = dot(ad, attw[:, CA : 3 * CA]).astype(BF16)
        return carry

    def filler(lo, hi):
        lax.fori_loop(lo, hi, kv_step, 0)

    start(3, 4, 5, 0, 1, 2)
    for load in loads[1:]:
        load.wait()
    arrived(3)
    start(7, 8)
    filler(0, 1)
    arrived(4)
    start(6)
    arrived(8)
    start(9)
    filler(1, 2)
    arrived(5, 6, 7, 9)
    start(10, 11, 13, 14, 16, 17)
    filler(2, 4)
    arrived(10)
    start(12, 18)
    arrived(14)
    start(15, 22)
    arrived(11)
    start(19)
    arrived(13)
    start(21)
    filler(4, 8)
    arrived(12)
    start(20)
    arrived(15)
    start(23)

    trunk = cond_own[...].astype(F32)
    trunk = jnp.concatenate([trunk + noise[k : k + 1, :] for k in range(4)], axis=0)
    cond_n = normalize(trunk).astype(BF16)
    m = dot(cond_n, modw[...])
    act = normalize(samp_own[...].astype(F32).reshape(32, CA))
    ad = (sigmoid(m[:, :CA]) * act + m[:, CA:]).astype(BF16)
    q_own[...] = dot(ad, attw[:, :CA]) * DH ** (-0.5)
    gate_own[...] = sigmoid(dot(ad, attw[:, 3 * CA :]))
    og_own[...] = sigmoid(dot(cond_n, ogw[...]))

    arrived(0, 1, 2, *range(16, 24))

    lane = lax.broadcasted_iota(jnp.int32, (128, 128), 1)

    def back(jp, d, e):
        dest = (r + d) % 4
        n = d * 2 + e - 1
        return pltpu.make_async_remote_copy(
            src_ref=gbuf.at[jp, dest],
            dst_ref=grecv.at[s, r, jp],
            send_sem=gssem.at[jp, n],
            recv_sem=grsem.at[jp, n],
            device_id=(dest, c, (s + e) % 2),
            device_id_type=MESH,
        )

    returns = [(d, e) for d in range(4) for e in range(2) if d + e > 0]

    def pair_step(jp, carry):
        for jj in range(2):
            x = cols[:, jp * 2 + jj].reshape(512, 128)
            qg = dot(x, wtri[:, :128])
            qbuf[...] = (qg * DT ** (-0.5)).astype(BF16)
            gatebuf[...] = sigmoid(qg)
            kvbuf[...] = dot(x, wtri[:, 128:]).astype(BF16)

            def chunk_step(ic, carry):
                rows = pl.ds(pl.multiple_of(ic * 128, 128), 128)
                q = qbuf[rows, :]
                parts = []
                for h in range(2):
                    qm = jnp.where((lane >= 32 * h) & (lane < 32 * h + 32), q, jnp.zeros_like(q))
                    add = jnp.concatenate(
                        [bias[pl.ds(ic * 4, 4), k, h].reshape(128, 128) for k in range(4)], axis=1
                    )
                    sc = dot_nt(qm, kvbuf[...]) + add
                    e = jnp.exp(sc - jnp.max(sc, axis=-1, keepdims=True))
                    total = jnp.sum(e, axis=-1, keepdims=True)
                    parts.append(dot(e.astype(BF16), kvbuf[...]) / total)
                res = jnp.where(lane < 96, parts[0], parts[1]) * gatebuf[rows, :]
                if jj == 0:
                    resbuf[rows, :] = pltpu.roll(res, 64, 1)
                else:
                    gbuf[jp, ic] = jnp.where(lane < 64, resbuf[rows, :], res).astype(BF16)
                return carry

            lax.fori_loop(0, 4, chunk_step, 0)
        for d, e in returns:
            back(jp, d, e).start()
        grecv[s, r, jp] = gbuf[jp, r]
        return carry

    lax.fori_loop(0, 4, pair_step, 0)

    def wait_step(jp, carry):
        for d, e in returns:
            back(jp, d, e).wait_recv()
        return carry

    lax.fori_loop(0, 4, wait_step, 0)

    def project_step(n, carry):
        src = n // 4
        jp = n % 4
        lhs = jnp.concatenate([grecv[0, src, jp], grecv[1, src, jp]], axis=1)
        out = dot(lhs, wo_big[...])
        f32buf[pl.ds(2 * n, 128, stride=32), :] = out[:, :128]
        f32buf[pl.ds(2 * n + 1, 128, stride=32), :] = out[:, 128:]
        return carry

    lax.fori_loop(0, 16, project_step, 0)

    def new_step(t, carry):
        x = pair_v[pl.ds(t * 8, 8)].astype(F32).reshape(256, 128)
        new = (x + f32buf[pl.ds(pl.multiple_of(t * 256, 256), 256), :]).astype(BF16)
        new_out[pl.ds(t * 8, 8)] = new.reshape(8, 32, 128)
        renorm[pl.ds(t * 8, 8)] = normalize(new).astype(BF16).reshape(8, 32, 128)
        return carry

    lax.fori_loop(0, 16, new_step, 0)

    acc = None
    for half in range(4):
        lhs = jnp.concatenate(
            [renorm[pl.ds(2 * half + k, 16, stride=8)].reshape(512, 128) for k in range(2)], axis=1
        )
        part = dot(lhs, pbw_big[256 * half : 256 * half + 256, :])
        acc = part if acc is None else acc + part
    pb_t[...] = acc.reshape(16, 32, 128)

    for d in range(1, 16):
        b = (c + d) % 16
        copies[23 + d] = send(23 + d, pb_t.at[b], pb_recv.at[c], col_peer(d))
        copies[23 + d].start()
    pb_recv[c] = pb_t[c]
    arrived(*range(24, 39))

    row_id = lax.broadcasted_iota(jnp.int32, (128, CA), 0)
    lane_id = lax.broadcasted_iota(jnp.int32, (128, CA), 1)
    head0 = (row_id % 16) * DH
    mask = (lane_id >= head0) & (lane_id < head0 + DH)

    def sample_step(k, carry):
        q = q_own[pl.ds(pl.multiple_of(k * 8, 8), 8), :]
        qb = jnp.broadcast_to(q[:, None, :], (8, 16, CA)).reshape(128, CA)
        qb = jnp.where(mask, qb, 0.0).astype(BF16)
        at = pl.ds(pl.multiple_of(k * 512, 512), 512)
        sc = dot_nt(kv_all[at, :CA], qb) + pb_recv[...].reshape(512, 128)
        e = jnp.exp(sc - jnp.max(sc, axis=0, keepdims=True))
        et = e.T
        total = jnp.sum(et, axis=-1, keepdims=True)
        out = dot(et.astype(BF16), kv_all[at, CA:]) / total
        out = jnp.where(mask, out, 0.0).reshape(8, 16, CA)
        att_all[pl.ds(pl.multiple_of(k * 8, 8), 8), :] = jnp.sum(out, axis=1)
        return carry

    lax.fori_loop(0, 4, sample_step, 0)
    gated = (gate_own[...] * att_all[...]).astype(BF16)
    upd_out[...] = (og_own[...] * dot(gated, ow[...])).astype(BF16).reshape(4, 8, CA)

    for n in range(39):
        copies[n].wait_send()

    def drain_step(jp, carry):
        for d, e in returns:
            back(jp, d, e).wait_send()
        return carry

    lax.fori_loop(0, 4, drain_step, 0)


def local(
    pair_repr,
    tri_weight,
    tri_bias_weight,
    tri_output_weight,
    samples,
    levels,
    single_cond,
    noise_weight,
    modulation_weight,
    attention_weight,
    pair_bias_weight,
    output_weight,
    output_gate_weight,
):
    s = lax.axis_index("smp")
    noise = jnp.dot(noise_features(levels).astype(BF16), noise_weight, preferred_element_type=F32)
    halves = lax.dynamic_slice_in_dim(tri_weight.reshape(128, 4, 2, 64), s, 1, 2)[:, :, 0]
    wtri = jnp.concatenate([halves[:, 0], halves[:, 3], halves[:, 1], halves[:, 2]], axis=1)
    tbw = jnp.pad(tri_bias_weight.T, ((0, 12), (0, 0)))
    zero = jnp.zeros((64, 128), BF16)
    wo_big = jnp.concatenate(
        [
            jnp.concatenate([tri_output_weight[64 * p : 64 * p + 64] if k == jj else zero for k in range(2)], axis=1)
            for p in range(2)
            for jj in range(2)
        ],
        axis=0,
    )
    eye = jnp.eye(8, dtype=BF16)
    pbw_big = (eye[:, None, :, None] * pair_bias_weight[None, :, None, :]).reshape(1024, 128)
    vm = pl.BlockSpec(memory_space=pltpu.VMEM)
    hbm = pl.BlockSpec(memory_space=pl.ANY)
    dma = pltpu.SemaphoreType.DMA
    return pl.pallas_call(
        kernel,
        out_shape=(
            jax.ShapeDtypeStruct((128, 32, 128), BF16),
            jax.ShapeDtypeStruct((4, 8, CA), BF16),
        ),
        in_specs=[vm] * 5 + [hbm] * 7,
        out_specs=(vm, vm),
        scratch_shapes=[
            pltpu.VMEM((128, 32, 128), BF16),
            pltpu.VMEM((4096, 128), F32),
            pltpu.VMEM((32, 128, 128), BF16),
            pltpu.VMEM((4, 32, 128), F32),
            pltpu.VMEM((4, 8, 128, 128), BF16),
            pltpu.VMEM((16, 4, 2, 32, 128), F32),
            pltpu.VMEM((512, 128), BF16),
            pltpu.VMEM((512, 128), BF16),
            pltpu.VMEM((512, 128), F32),
            pltpu.VMEM((512, 128), F32),
            pltpu.VMEM((4, 4, 128, 128), BF16),
            pltpu.VMEM((2, 4, 4, 128, 128), BF16),
            pltpu.VMEM((128, 32, 128), BF16),
            pltpu.VMEM((16, 32, 128), F32),
            pltpu.VMEM((16, 32, 128), F32),
            pltpu.VMEM((4, 512, CA), BF16),
            pltpu.VMEM((512, 384), BF16),
            pltpu.VMEM((4, 8, CA), BF16),
            pltpu.VMEM((8, 384), BF16),
            pltpu.VMEM((384, 2 * CA), BF16),
            pltpu.VMEM((CA, 4 * CA), BF16),
            pltpu.VMEM((CA, CA), BF16),
            pltpu.VMEM((384, CA), BF16),
            pltpu.VMEM((2048, 2 * CA), BF16),
            pltpu.VMEM((32, CA), F32),
            pltpu.VMEM((32, CA), F32),
            pltpu.VMEM((32, CA), F32),
            pltpu.VMEM((32, CA), F32),
            dma((9,)),
            dma((39,)),
            dma((39,)),
            dma((4, 7)),
            dma((4, 7)),
        ],
        compiler_params=pltpu.CompilerParams(
            collective_id=0, has_side_effects=True, vmem_limit_bytes=62 * 1024 * 1024
        ),
        name="pair_and_samples",
    )(
        noise,
        wtri,
        tbw,
        wo_big,
        pbw_big,
        pair_repr,
        samples,
        single_cond,
        modulation_weight,
        attention_weight,
        output_weight,
        output_gate_weight,
    )


def solution(mesh):
    return jax.shard_map(
        local,
        mesh=mesh,
        in_specs=(
            P("row", "col", None),
            P(),
            P(),
            P(),
            P("smp", None, None),
            P("smp"),
            P(),
            P(),
            P(),
            P(),
            P(),
            P(),
            P(),
        ),
        out_specs=(P("row", "col", None), P("smp", ("row", "col"), None)),
        check_vma=False,
    )
```

time: 463 us -> 110 us (0.24)
  waiting for transfers between devices: 134 us -> 0 us
  Pallas kernels: 0 us -> 97.7 us
  local copies, waits for them, and re-layouts: 103 us -> 7.84 us
  other arithmetic: 77.4 us -> 3 us
  blocking collectives: 59.1 us -> 0 us
  matrix products: 49.2 us -> 0.74 us
  loops' own time: 16.2 us -> 0 us
  between operations: 14.5 us -> 0.71 us
  starting transfers between devices: 8.01 us -> 0 us
    all_gather x2 -> x0, waiting for transfers between devices: 129 us -> none  [the longest x1 98.4 us: combined_all(): gathered = jax.tree.map(lambda a: lax.all_gather(a, axis), part)]
    pallas_call x0 -> x1, Pallas kernels: none -> 97.7 us  [local(): pl.pallas_call(kernel, out_shape=(jax.ShapeDtypeStruct((128, 32, 128), BF...]
    dynamic_slice x96 -> x2, local copies, waits for them, and re-layouts: 61.3 us -> 0.14 us  [local(): lax.dynamic_slice_in_dim(tri_weight.reshape(128, 4, 2, 64), s, 1, 2)]
    all_gather x3 -> x0, blocking collectives: 59.1 us -> none  [the longest x2 46.8 us: combined_all(): gathered = jax.tree.map(lambda a: lax.all_gather(a, axis), part)]
    dot_general x29 -> x1, matrix products: 49.2 us -> 0.74 us  [local(): jnp.dot(noise_features(levels).astype(BF16), noise_weight, preferred_elem...]
    add x15 -> x0, other arithmetic: 43.6 us -> none  [combine_parts(): rescale(sum_one, factor_one) + rescale(sum_two, factor_two)]
    while x138 -> x0, local copies, waits for them, and re-layouts: 22.6 us -> none
    reduce_sum x23 -> x0, other arithmetic: 18.9 us -> none  [the longest x7 8.01 us: normalize(): variance = jnp.mean(centred * centred, axis=-1, keepdims=True)]
  transfers between devices with their start and end apart: 4 -> 0, of which waited for: 3 -> 0; matrix products, arithmetic and copies ran while one was open for 7% -> 0% of each run, Pallas kernels for 0% -> 0%
where the time goes in v1:
time: 110 us
  Pallas kernels  97.7 us (89%)
  local copies, waits for them, and re-layouts  7.84 us (7%)
  other arithmetic  3 us (3%)
    pallas_call x1, Pallas kernels, local(): pl.pallas_call(kernel, out_shape=(jax.ShapeDtypeStruct((128, 32, 128), BF...  97.7 us
    unnamed x6, local copies, waits for them, and re-layouts  4.83 us

profile of v1, /device:TPU:1, one launch (start us, length us, event | category | flops | bytes accessed | tf_op | source)
XLA Modules:
  0.0 110.0 jit_solution(14785119848122907347)
XLA Ops:
  0.6 0.0 copy-start
  0.6 0.7 fusion.18
  1.4 0.1 fusion.10
  1.5 0.1 copy-done
  1.6 0.7 fusion.12.noise
  2.3 1.3 %pad.8.tbw = bf16[16,128]{1,0:T(8,128)(2,1)} pad(bf16[4,128]{1,0:T(4,128)(2,1)} %bitcast.23, bf16[]{:T(256)} %constant.26.clone.1), padding=0_12x0_0 | pad | bytes 5122 | tf_op jit(solution)/shard_map/jit(_pad)/pad | solution.py:436
  3.6 0.7 fusion.20
  4.3 0.7 fusion.7.wo_big
  5.0 1.0 copy.17
  6.0 0.1 copy.18
  6.2 0.7 pad_maximum_fusion.wtri
  6.9 0.8 broadcast_multiply_fusion
  7.7 0.8 copy.19.pbw_big
  8.6 97.7 %pair_and_samples.1 = (bf16[128,32,128]{2,1,0:T(8,128)(2,1)}, bf16[4,8,768]{2,1,0:T(8,128)(2,1)}) custom-call(f32[4,384]{1,0:T(4,128)} %fusion.12.noise, bf16[128,256]{1,0:T(8,128)(2,1)} %pad_maximum_fusion.wtri, bf16[16,128]{1,0:T(8,128)(2,1)} %pad.8.tbw, bf16[256,256]{1,0:T(8,128)(2,1)} %fusion.7.wo_big, bf16[1024,128]{1,0:T(8,128)(2,1)} %copy.19.pbw_big, ...), custom_call_target="tpu_custom_call" | custom-call | tf_op jit(solution)/shard_map/pair_and_samples/pallas_call | solution.py:451
  106.3 2.3 %copy.25 = bf16[128,32,128]{2,1,0:T(8,128)(2,1)} copy(bf16[128,32,128]{2,1,0:T(8,128)(2,1)} %get-tuple-element.12) | data formatting | bytes 2097152
  108.5 1.4 %copy.26 = bf16[4,8,768]{2,1,0:T(8,128)(2,1)} copy(bf16[4,8,768]{2,1,0:T(8,128)(2,1)} %get-tuple-element.13) | data formatting | bytes 98304
  (5 shorter events, 0.1 us)
Async XLA Ops:
  0.6 0.9 copy-start
